TPU v7x, 512 devices: a whole 4x8x8 slice. The times are simulated.
512 devices in a mesh: shard: 64 (over x, z, core), rep: 8 (over y).
Axes of the slice: x: 4, y: 8, z: 8, core: 2. Of those that a mesh axis runs over, the one named last changes fastest.
Arguments:
- attn_grad: bfloat16 [8, 2, 4, 768, 768], P('rep', None, None, 'shard'), may hold values from -16 to 16
- attn_error: float32 [8, 2, 4, 768, 768], P('rep', None, None, 'shard'), may hold values from -6 to 6
- attn_basis: float32 [2, 4, 768, 32], P(None, None, 'shard'), may hold values from -0.21875 to 0.21875
- attn_roots: float32 [2, 4, 3, 32, 32], replicated, as said below
- attn_momentum: float32 [2, 4, 768, 768], P(None, None, 'shard'), may hold values from -4 to 4
- attn_weights: float32 [2, 4, 768, 768], P(None, None, 'shard'), may hold values from -0.21875 to 0.21875
- mlp_grad: bfloat16 [8, 2, 2, 768, 3072], P('rep', None, None, 'shard'), may hold values from -16 to 16
- mlp_error: float32 [8, 2, 2, 768, 3072], P('rep', None, None, 'shard'), may hold values from -6 to 6
- mlp_basis: float32 [2, 2, 3072, 32], P(None, None, 'shard'), may hold values from -0.109375 to 0.109375
- mlp_roots: float32 [2, 2, 3, 32, 32], replicated, as said below
- mlp_momentum: float32 [2, 2, 768, 3072], P(None, None, 'shard'), may hold values from -4 to 4
- mlp_weights: float32 [2, 2, 768, 3072], P(None, None, 'shard'), may hold values from -0.21875 to 0.21875
- small_grad: bfloat16 [8, 2, 9984], P('rep', None, 'shard'), may hold values from -6 to 6
- small_momentum: float32 [2, 9984], P(None, 'shard'), may hold values from -4 to 4
- small_weights: float32 [2, 9984], P(None, 'shard'), may hold values from -6 to 6
Outputs:
- attn_error_out: float32 [8, 2, 4, 768, 768], P('rep', None, None, 'shard')
- mlp_error_out: float32 [8, 2, 2, 768, 3072], P('rep', None, None, 'shard')
- attn_left: float32 [2, 4, 768, 32], P(None, None, 'shard')
- attn_right: float32 [2, 4, 768, 32], P(None, None, 'shard')
- mlp_left: float32 [2, 2, 768, 32], P(None, None, 'shard')
- mlp_right: float32 [2, 2, 3072, 32], P(None, None, 'shard')
- attn_momentum_out: float32 [2, 4, 768, 768], P(None, None, 'shard')
- attn_weights_out: float32 [2, 4, 768, 768], P(None, None, 'shard')
- mlp_momentum_out: float32 [2, 2, 768, 3072], P(None, None, 'shard')
- mlp_weights_out: float32 [2, 2, 768, 3072], P(None, None, 'shard')
- small_momentum_out: float32 [2, 9984], P(None, 'shard')
- small_weights_out: float32 [2, 9984], P(None, 'shard')
Inputs may be any that keep to these rules, and one draw needn't show every extreme that they name: Every 32 x 32 factor of attn_roots is a scaled identity plus independent entries and is well conditioned. Every 32 x 32 factor of mlp_roots is a scaled identity plus independent entries and is well conditioned.
All inputs are finite; a program needn't handle non-finite values.
Results may differ from a plain program's by a relative error of at most 0.0003.
Values sent between devices are 32-bit elements; how exact they have to be, the bound alone decides.
A program may use at most 64 MiB of HBM per device.

v0:
```python
import jax
import jax.numpy as jnp
from jax import lax
from jax.sharding import PartitionSpec as P

momentum_decay = 0.9
learn_rate = 0.05


def rows_product(merged, factor):
    return jnp.einsum("lkrc,lkcn->lkrn", merged, factor, precision=lax.Precision.HIGHEST)


def cols_product(merged, factor):
    return jnp.einsum("lkrc,lkrn->lkcn", merged, factor, precision=lax.Precision.HIGHEST)


def rotate(factor, inverse_roots, round_index):
    return jnp.einsum(
        "lkrn,lknm->lkrm", factor, inverse_roots[:, :, round_index], precision=lax.Precision.HIGHEST
    )


def finish(summed, inverse_roots, round_index):
    if round_index < 0:
        return summed / float(lax.axis_size("rep"))
    return rotate(summed, inverse_roots, round_index)


def own_share(full_factor):
    share_width = full_factor.shape[2] // lax.axis_size("shard")
    share_start = lax.axis_index("shard") * share_width
    return lax.dynamic_slice_in_dim(full_factor, share_start, share_width, 2)


def column_round(attn_term, mlp_term, attn_roots, mlp_roots, round_index):
    attn_full, mlp_full = lax.psum((attn_term, mlp_term), ("shard", "rep"))
    attn_full = finish(attn_full, attn_roots, round_index)
    mlp_full = finish(mlp_full, mlp_roots, round_index)
    attn_share = own_share(attn_full)
    mlp_share = own_share(mlp_full)
    attn_next, mlp_next = (attn_full, mlp_full)
    return (attn_next, mlp_next, attn_full, mlp_full, attn_share, mlp_share)


def update(merged, approx, momentum, weights):
    error_out = (merged - approx)[None]
    momentum_out = momentum_decay * momentum + approx
    weights_out = weights - learn_rate * momentum_out
    return (error_out, momentum_out, weights_out)


def per_device(
    attn_grad,
    attn_error,
    attn_basis,
    attn_roots,
    attn_momentum,
    attn_weights,
    mlp_grad,
    mlp_error,
    mlp_basis,
    mlp_roots,
    mlp_momentum,
    mlp_weights,
    small_grad,
    small_momentum,
    small_weights,
):
    attn_merged = attn_grad[0].astype(jnp.float32) + attn_error[0]
    mlp_merged = mlp_grad[0].astype(jnp.float32) + mlp_error[0]
    small_local = small_grad[0].astype(jnp.float32)
    attn_bfull, mlp_bfull = (
        lax.all_gather(attn_basis, "shard", axis=2, tiled=True),
        lax.all_gather(mlp_basis, "shard", axis=2, tiled=True),
    )
    attn_data, mlp_data = (attn_merged, mlp_merged)
    attn_start, mlp_start = (attn_bfull, mlp_bfull)
    attn_first = rows_product(attn_data, attn_start)
    mlp_first = rows_product(mlp_data, mlp_start)
    small_total = lax.psum(small_local, "rep")
    attn_first, mlp_first = lax.psum((attn_first, mlp_first), "rep")
    attn_lhat = rotate(attn_first, attn_roots, 0)
    mlp_lhat = rotate(mlp_first, mlp_roots, 0)
    attn_rhat, mlp_rhat, spare_one, spare_two, spare_three, spare_four = column_round(
        cols_product(attn_data, attn_lhat),
        cols_product(mlp_data, mlp_lhat),
        attn_roots,
        mlp_roots,
        1,
    )
    attn_second, mlp_second = lax.psum(
        (rows_product(attn_data, attn_rhat), rows_product(mlp_data, mlp_rhat)), "rep"
    )
    attn_left = rotate(attn_second, attn_roots, 2)
    mlp_left = rotate(mlp_second, mlp_roots, 2)
    spare_five, spare_six, attn_rfull, mlp_rfull, attn_right, mlp_right = column_round(
        cols_product(attn_data, attn_left),
        cols_product(mlp_data, mlp_left),
        attn_roots,
        mlp_roots,
        -1,
    )
    attn_approx = jnp.einsum(
        "lkrn,lkcn->lkrc", attn_left, attn_rfull, precision=lax.Precision.HIGHEST
    )
    mlp_approx = jnp.einsum("lkrn,lkcn->lkrc", mlp_left, mlp_rfull, precision=lax.Precision.HIGHEST)
    attn_error_out, attn_momentum_out, attn_weights_out = update(
        attn_merged, attn_approx, attn_momentum, attn_weights
    )
    mlp_error_out, mlp_momentum_out, mlp_weights_out = update(
        mlp_merged, mlp_approx, mlp_momentum, mlp_weights
    )
    small_mean = small_total / float(lax.axis_size("rep"))
    small_momentum_out = momentum_decay * small_momentum + small_mean
    small_weights_out = small_weights - learn_rate * small_momentum_out
    return (
        attn_error_out,
        mlp_error_out,
        attn_left,
        attn_right,
        mlp_left,
        mlp_right,
        attn_momentum_out,
        attn_weights_out,
        mlp_momentum_out,
        mlp_weights_out,
        small_momentum_out,
        small_weights_out,
    )


def solution(mesh):
    in_specs = (
        P("rep", None, None, "shard", None),
        P("rep", None, None, "shard", None),
        P(None, None, "shard", None),
        P(),
        P(None, None, "shard", None),
        P(None, None, "shard", None),
        P("rep", None, None, "shard", None),
        P("rep", None, None, "shard", None),
        P(None, None, "shard", None),
        P(),
        P(None, None, "shard", None),
        P(None, None, "shard", None),
        P("rep", None, "shard"),
        P(None, "shard"),
        P(None, "shard"),
    )
    out_specs = (
        P("rep", None, None, "shard", None),
        P("rep", None, None, "shard", None),
        P(None, None, "shard", None),
        P(None, None, "shard", None),
        P(None, None, "shard", None),
        P(None, None, "shard", None),
        P(None, None, "shard", None),
        P(None, None, "shard", None),
        P(None, None, "shard", None),
        P(None, None, "shard", None),
        P(None, "shard"),
        P(None, "shard"),
    )
    return jax.shard_map(
        per_device, mesh=mesh, in_specs=in_specs, out_specs=out_specs, check_vma=False
    )
```

profile of v0, /device:TPU:1, one launch (start us, length us, event | category | flops | bytes accessed | tf_op | source)
XLA Modules:
  0.0 757.0 jit_solution(16800400785792100691)
XLA Ops:
  7.2 0.0 all-gather.2.cloned.1.call-start
  7.2 1.6 copy.101
  8.8 0.0 all-gather.2.cloned.1.call-update
  8.8 0.0 all-reduce.9.cloned.1.call-start
  8.9 0.8 copy.94
  9.7 0.0 copy-start.2
  9.7 0.0 copy-start.3
  9.7 59.7 %all_gather.6 = f32[2,4,768,32]{3,1,0,2:T(4,128)S(1)} all-gather(f32[2,4,12,32]{3,1,0,2:T(4,128)S(1)} %copy.94), channel_id=1, replica_groups=mesh['shard'=64,'rep'=8] {'shard'}, dimensions={2}, use_global_device_ids=true | all-gather | bytes 798720 | tf_op jit(solution)/shard_map/all_gather | solution.py:74
  69.4 0.0 copy-done.2
  69.4 0.0 copy-done.3
  69.4 0.0 copy-start
  69.4 0.0 copy-start.1
  69.4 2.1 fusion.2
  71.5 0.0 copy-start.11
  71.6 33.6 %all-gather.2.cloned.1.call-done = f32[2,2,3072,32]{3,1,0,2:T(2,128)} async-done(((f32[2,2,48,32]{3,1,0,2:T(2,128)}), f32[2,2,3072,32]{3,1,0,2:T(2,128)}) %all-gather.2.cloned.1.call-update) | async-done | bytes 1572880 | tf_op jit(solution)/shard_map/all_gather | solution.py:75
  105.2 0.0 copy-done
  105.2 0.0 copy-done.1
  105.2 6.1 fusion
  111.3 0.0 copy-start.12
  111.3 23.7 %all-reduce.3 = (f32[2,4,12,32]{3,2,1,0:T(8,128)S(1)}, f32[2,2,12,32]{3,2,1,0:T(8,128)S(1)}) all-reduce(f32[2,4,12,32]{3,2,1,0:T(8,128)S(1)} %fusion.2, f32[2,2,12,32]{3,2,1,0:T(8,128)S(1)} %fusion), channel_id=1, replica_groups=mesh['shard'=64,'rep'=8] {'rep'}, use_global_device_ids=true, to_apply=%region_0.0 | all-reduce | flops 4608 | bytes 36864 | tf_op jit(solution)/shard_map/psum | solution.py:82
  135.1 0.0 copy-done.11
  135.1 0.2 fusion.26
  135.3 1.7 fusion.17
  137.0 0.0 copy-done.12
  137.0 0.2 fusion.35
  137.2 2.8 fusion.8
  140.0 0.0 all-reduce.9.cloned.1.call-update
  140.0 0.2 all-reduce.7.cloned.1.call-start
  140.3 0.4 copy-done.15
  140.7 279.9 %all-reduce.9.cloned.1.call-done = (f32[2,4,768,32]{2,3,1,0:T(8,128)}, f32[2,2,3072,32]{2,3,1,0:T(8,128)}) async-done(((f32[2,4,768,32]{2,3,1,0:T(8,128)}, f32[2,2,3072,32]{2,3,1,0:T(8,128)}), (f32[2,4,768,32]{2,3,1,0:T(8,128)}, f32[2,2,3072,32]{2,3,1,0:T(8,128)})) %all-reduce.9.cloned.1.call-update) | async-done | bytes 2359312 | tf_op jit(solution)/shard_map/psum | solution.py:37
  420.6 2.1 fusion.22
  422.7 0.8 fusion.15
  423.5 1.5 fusion.31
  424.9 1.6 fusion.6
  426.6 23.4 %all-reduce.2 = (f32[2,4,12,32]{3,2,1,0:T(8,128)S(1)}, f32[2,2,12,32]{3,2,1,0:T(8,128)S(1)}, f32[2,156]{1,0:T(2,128)S(1)}) all-reduce(f32[2,4,12,32]{3,2,1,0:T(8,128)S(1)} %fusion.15, f32[2,2,12,32]{3,2,1,0:T(8,128)S(1)} %fusion.6, f32[2,156]{1,0:T(2,128)S(1)} %bitcast_convert_fusion), channel_id=1, replica_groups=mesh['shard'=64,'rep'=8] {'rep'}, use_global_device_ids=true, to_apply=%region_2.0 | all-reduce | flops 4920 | bytes 39360 | tf_op jit(solution)/shard_map/psum | solution.py:92
  450.0 0.2 fusion.24
  450.2 0.2 fusion.33
  450.4 1.7 fusion.13
  452.1 2.8 fusion.4
  454.9 0.0 all-reduce.7.cloned.1.call-update
  454.9 0.0 copy-start.9
  454.9 0.0 copy-start.10
  454.9 0.6 copy.114
  455.6 0.6 copy.112
  456.2 0.0 copy-done.14
  456.2 0.6 multiply_subtract_fusion
  456.8 280.8 %all-reduce.7.cloned.1.call-done = (f32[2,4,768,32]{2,3,1,0:T(8,128)}, f32[2,2,3072,32]{2,3,1,0:T(8,128)}) async-done(((f32[2,4,768,32]{2,3,1,0:T(8,128)}, f32[2,2,3072,32]{2,3,1,0:T(8,128)}), (f32[2,4,768,32]{2,3,1,0:T(8,128)}, f32[2,2,3072,32]{2,3,1,0:T(8,128)})) %all-reduce.7.cloned.1.call-update) | async-done | bytes 2359312 | tf_op jit(solution)/shard_map/psum | solution.py:37
  737.6 1.3 broadcast_multiply_fusion.1
  738.9 0.1 constant_dynamic-slice_fusion.1
  739.0 0.7 copy.113
  739.7 0.0 copy-done.9
  739.7 0.0 copy-done.5
  739.7 0.7 copy_subtract_fusion.1
  740.4 0.9 copy.116
  741.3 0.9 copy.115
  742.2 0.9 copy.110
  743.1 0.1 broadcast_multiply_fusion
  743.3 0.9 copy-done.7
  744.2 0.2 copy-done.8
  744.4 1.5 copy_subtract_fusion
  745.9 1.3 copy.118
  747.2 1.3 copy.117
  748.5 1.3 copy.111
  749.7 0.7 constant_dynamic-slice_fusion
  (13 shorter events, 0.0 us)
Async XLA Ops:
  7.2 98.0 %all-gather.2.cloned.1.call-start = ((), (), s32[]{:S(2)}) async-start(), calls=%async_computation | async-start | bytes 6389760 | tf_op jit(solution)/shard_map/all_gather | solution.py:75
  8.8 411.8 %all-reduce.9.cloned.1.call-start = ((), (), s32[]{:S(2)}) async-start(), calls=%async_computation.2 | async-start | bytes 4718592 | tf_op jit(solution)/shard_map/psum | solution.py:37
  9.7 59.7 %copy-start.2 = (f32[1,2,4,12,768]{4,2,3,1,0:T(4,128)S(1)}, f32[1,2,4,12,768]{4,2,3,1,0:T(4,128)}, u32[]{:S(2)}) copy-start(f32[1,2,4,12,768]{4,2,3,1,0:T(4,128)} %param.16) | copy-start | bytes 884740
  9.7 59.7 %copy-start.3 = (bf16[1,2,4,12,768]{4,2,3,1,0:T(4,128)(2,1)S(1)}, bf16[1,2,4,12,768]{4,2,3,1,0:T(4,128)(2,1)}, u32[]{:S(2)}) copy-start(bf16[1,2,4,12,768]{4,2,3,1,0:T(4,128)(2,1)} %param.15) | copy-start | bytes 442372
  69.4 35.8 %copy-start = (f32[1,2,2,12,3072]{4,2,3,1,0:T(2,128)S(1)}, f32[1,2,2,12,3072]{4,2,3,1,0:T(2,128)}, u32[]{:S(2)}) copy-start(f32[1,2,2,12,3072]{4,2,3,1,0:T(2,128)} %param.22) | copy-start | bytes 1769476
  69.4 35.8 %copy-start.1 = (bf16[1,2,2,12,3072]{4,2,3,1,0:T(2,128)(2,1)S(1)}, bf16[1,2,2,12,3072]{4,2,3,1,0:T(2,128)(2,1)}, u32[]{:S(2)}) copy-start(bf16[1,2,2,12,3072]{4,2,3,1,0:T(2,128)(2,1)} %param.21) | copy-start | bytes 884740
  71.5 63.5 %copy-start.11 = (f32[2,4,3,32,32]{4,3,2,1,0:T(8,128)S(1)}, f32[2,4,3,32,32]{4,3,2,1,0:T(8,128)}, u32[]{:S(2)}) copy-start(f32[2,4,3,32,32]{4,3,2,1,0:T(8,128)} %param.18) | copy-start | bytes 294916
  111.3 25.7 %copy-start.12 = (f32[2,2,3,32,32]{4,3,2,1,0:T(8,128)S(1)}, f32[2,2,3,32,32]{4,3,2,1,0:T(8,128)}, u32[]{:S(2)}) copy-start(f32[2,2,3,32,32]{4,3,2,1,0:T(8,128)} %param.24) | copy-start | bytes 147460
  140.0 0.7 copy-start.15
  140.0 597.6 %all-reduce.7.cloned.1.call-start = ((), (), s32[]{:S(2)}) async-start(), calls=%async_computation.1 | async-start | bytes 4718592 | tf_op jit(solution)/shard_map/psum | solution.py:37
  420.6 2.9 copy-start.6
  454.9 1.3 copy-start.13
  454.9 1.3 copy-start.14
  454.9 284.8 %copy-start.9 = (f32[2,4,12,768]{3,1,2,0:T(4,128)S(1)}, f32[2,4,12,768]{3,1,2,0:T(4,128)}, u32[]{:S(2)}) copy-start(f32[2,4,12,768]{3,1,2,0:T(4,128)} %param.20) | copy-start | bytes 884740
  454.9 284.8 %copy-start.10 = (f32[2,4,12,768]{3,1,2,0:T(4,128)S(1)}, f32[2,4,12,768]{3,1,2,0:T(4,128)}, u32[]{:S(2)}) copy-start(f32[2,4,12,768]{3,1,2,0:T(4,128)} %param.19) | copy-start | bytes 884740
  737.6 2.1 copy-start.5
  740.4 2.7 copy-start.4
  743.1 1.1 copy-start.7
  743.1 1.2 copy-start.8
Sparse Core Ops, SparseCore 0:
  11.9 93.1 all-gather.1
  140.1 280.3 all-reduce.8
  455.0 282.5 all-reduce.6
where the time goes:
time: 757 us
  waiting for transfers between devices  594 us (78%)
  blocking collectives  107 us (14%)
  matrix products  26.2 us (3%)
  between operations  14 us (2%)
  local copies, waits for them, and re-layouts  13.3 us (2%)
    psum x2, waiting for transfers between devices, column_round(): attn_full, mlp_full = lax.psum((attn_term, mlp_term), ('shard', 'rep'))  561 us
    all_gather x1, blocking collectives, per_device(): lax.all_gather(attn_basis, 'shard', axis=2, tiled=True)  59.7 us
    all_gather x1, waiting for transfers between devices, per_device(): lax.all_gather(mlp_basis, 'shard', axis=2, tiled=True)  33.6 us
    psum x1, blocking collectives, per_device(): attn_first, mlp_first = lax.psum((attn_first, mlp_first), 'rep')  23.7 us
    psum x1, blocking collectives, per_device(): lax.psum((rows_product(attn_data, attn_rhat), rows_product(mlp_data, mlp_...  23.4 us
  transfers between devices with their start and end apart: 3, of which 3 were waited for; matrix products, arithmetic and copies ran while one was open for 1% of the time, Pallas kernels for 0%

commit v1 on v0

--- a/solution.py
+++ b/solution.py
@@ -34,7 +34,7 @@
 
 
 def column_round(attn_term, mlp_term, attn_roots, mlp_roots, round_index):
-    attn_full, mlp_full = lax.psum((attn_term, mlp_term), ("shard", "rep"))
+    attn_full, mlp_full = lax.psum(lax.psum((attn_term, mlp_term), "rep"), "shard")
     attn_full = finish(attn_full, attn_roots, round_index)
     mlp_full = finish(mlp_full, mlp_roots, round_index)
     attn_share = own_share(attn_full)

time: 757 us -> 785 us (1.037)
  waiting for transfers between devices: 594 us -> 621 us
    psum x2 -> x4, waiting for transfers between devices: 561 us -> 587 us  [the longest x2 410 us: column_round(): lax.psum(lax.psum((attn_term, mlp_term), 'rep'), 'shard')]
  transfers between devices with their start and end apart: 3 -> 5, of which waited for: 3 -> 5; matrix products, arithmetic and copies ran while one was open for 1% -> 1% of each run, Pallas kernels for 0% -> 0%
where the time goes in v1:
time: 785 us; the launch traced here: 784 us
  waiting for transfers between devices  621 us (79%)
  blocking collectives  108 us (14%)
  matrix products  26.2 us (3%)
  between operations  14 us (2%)
  local copies, waits for them, and re-layouts  12.9 us (2%)
    psum x2, waiting for transfers between devices, column_round(): lax.psum(lax.psum((attn_term, mlp_term), 'rep'), 'shard')  410 us
    psum x2, waiting for transfers between devices, column_round(): lax.psum((attn_term, mlp_term), 'rep')  177 us
    all_gather x1, blocking collectives, per_device(): lax.all_gather(attn_basis, 'shard', axis=2, tiled=True)  59.7 us
    all_gather x1, waiting for transfers between devices, per_device(): lax.all_gather(mlp_basis, 'shard', axis=2, tiled=True)  33.6 us
    psum x1, blocking collectives, per_device(): lax.psum((rows_product(attn_data, attn_rhat), rows_product(mlp_data, mlp_...  24.6 us
    psum x1, blocking collectives, per_device(): attn_first, mlp_first = lax.psum((attn_first, mlp_first), 'rep')  23.7 us
  transfers between devices with their start and end apart: 5, of which 5 were waited for; matrix products, arithmetic and copies ran while one was open for 1% of the time, Pallas kernels for 0%

profile of v1, /device:TPU:1, one launch (start us, length us, event | category | flops | bytes accessed | tf_op | source)
XLA Modules:
  0.0 784.4 jit_solution(6959431743188502121)
XLA Ops:
  7.2 0.0 all-gather.2.cloned.1.call-start
  7.2 1.6 copy.101
  8.8 0.0 all-gather.2.cloned.1.call-update
  8.8 0.0 all-reduce.17.cloned.1.call-start
  8.9 0.8 copy.94
  9.7 0.0 copy-start.2
  9.7 0.0 copy-start.3
  9.7 59.7 %all_gather.6 = f32[2,4,768,32]{3,1,0,2:T(4,128)S(1)} all-gather(f32[2,4,12,32]{3,1,0,2:T(4,128)S(1)} %copy.94), channel_id=1, replica_groups=mesh['shard'=64,'rep'=8] {'shard'}, dimensions={2}, use_global_device_ids=true | all-gather | bytes 798720 | tf_op jit(solution)/shard_map/all_gather | solution.py:74
  69.4 0.0 copy-start
  69.4 0.0 copy-start.1
  69.4 2.1 fusion.2
  71.5 0.0 copy-start.11
  71.6 33.6 %all-gather.2.cloned.1.call-done = f32[2,2,3072,32]{3,1,0,2:T(2,128)} async-done(((f32[2,2,48,32]{3,1,0,2:T(2,128)}), f32[2,2,3072,32]{3,1,0,2:T(2,128)}) %all-gather.2.cloned.1.call-update) | async-done | bytes 1572880 | tf_op jit(solution)/shard_map/all_gather | solution.py:75
  105.2 6.1 fusion
  111.3 0.0 copy-start.12
  111.3 23.7 %all-reduce.3 = (f32[2,4,12,32]{3,2,1,0:T(8,128)S(1)}, f32[2,2,12,32]{3,2,1,0:T(8,128)S(1)}) all-reduce(f32[2,4,12,32]{3,2,1,0:T(8,128)S(1)} %fusion.2, f32[2,2,12,32]{3,2,1,0:T(8,128)S(1)} %fusion), channel_id=1, replica_groups=mesh['shard'=64,'rep'=8] {'rep'}, use_global_device_ids=true, to_apply=%region_0.0 | all-reduce | flops 4608 | bytes 36864 | tf_op jit(solution)/shard_map/psum | solution.py:82
  135.1 0.0 copy-done.11
  135.1 0.2 fusion.26
  135.3 1.7 fusion.17
  137.0 0.2 fusion.35
  137.2 2.8 fusion.8
  140.0 0.0 all-reduce.17.cloned.1.call-update
  140.0 0.0 copy-start.15
  140.0 0.0 all-reduce.13.cloned.1.call-start
  140.1 86.9 %all-reduce.17.cloned.1.call-done = (f32[2,4,768,32]{2,3,1,0:T(8,128)}, f32[2,2,3072,32]{2,3,1,0:T(8,128)}) async-done(((f32[2,4,768,32]{2,3,1,0:T(8,128)}, f32[2,2,3072,32]{2,3,1,0:T(8,128)}), (f32[2,4,768,32]{2,3,1,0:T(8,128)}, f32[2,2,3072,32]{2,3,1,0:T(8,128)})) %all-reduce.17.cloned.1.call-update) | async-done | bytes 2359312 | tf_op jit(solution)/shard_map/psum | solution.py:37
  227.0 0.0 all-reduce.13.cloned.1.call-update
  227.0 0.2 all-reduce.15.cloned.1.call-start
  227.3 206.0 %all-reduce.13.cloned.1.call-done = (f32[2,4,768,32]{2,3,1,0:T(8,128)}, f32[2,2,3072,32]{2,3,1,0:T(8,128)}) async-done(((f32[2,4,768,32]{2,3,1,0:T(8,128)}, f32[2,2,3072,32]{2,3,1,0:T(8,128)}), (f32[2,4,768,32]{2,3,1,0:T(8,128)}, f32[2,2,3072,32]{2,3,1,0:T(8,128)})) %all-reduce.13.cloned.1.call-update) | async-done | bytes 2359312 | tf_op jit(solution)/shard_map/psum | solution.py:37
  433.3 2.1 fusion.22
  435.4 0.8 fusion.15
  436.2 1.5 fusion.31
  437.7 1.6 fusion.6
  439.3 24.6 %all-reduce.2 = (f32[2,4,12,32]{3,2,1,0:T(8,128)S(1)}, f32[2,2,12,32]{3,2,1,0:T(8,128)S(1)}, f32[2,156]{1,0:T(2,128)S(1)}) all-reduce(f32[2,4,12,32]{3,2,1,0:T(8,128)S(1)} %fusion.15, f32[2,2,12,32]{3,2,1,0:T(8,128)S(1)} %fusion.6, f32[2,156]{1,0:T(2,128)S(1)} %bitcast_convert_fusion), channel_id=1, replica_groups=mesh['shard'=64,'rep'=8] {'rep'}, use_global_device_ids=true, to_apply=%region_3.0 | all-reduce | flops 4920 | bytes 39360 | tf_op jit(solution)/shard_map/psum | solution.py:92
  463.9 0.2 fusion.24
  464.1 0.2 fusion.33
  464.3 1.7 fusion.13
  466.0 2.8 fusion.4
  468.8 0.0 all-reduce.15.cloned.1.call-update
  468.8 0.0 copy-start.13
  468.8 0.0 copy-start.14
  468.8 0.3 all-reduce.11.cloned.1.call-start
  469.1 89.9 %all-reduce.15.cloned.1.call-done = (f32[2,4,768,32]{2,3,1,0:T(8,128)}, f32[2,2,3072,32]{2,3,1,0:T(8,128)}) async-done(((f32[2,4,768,32]{2,3,1,0:T(8,128)}, f32[2,2,3072,32]{2,3,1,0:T(8,128)}), (f32[2,4,768,32]{2,3,1,0:T(8,128)}, f32[2,2,3072,32]{2,3,1,0:T(8,128)})) %all-reduce.15.cloned.1.call-update) | async-done | bytes 2359312 | tf_op jit(solution)/shard_map/psum | solution.py:37
  558.9 0.0 all-reduce.11.cloned.1.call-update
  559.0 0.0 copy-start.9
  559.0 0.0 copy-start.10
  559.0 0.6 copy.114
  559.6 0.6 copy.112
  560.3 0.6 multiply_subtract_fusion
  560.9 204.2 %all-reduce.11.cloned.1.call-done = (f32[2,4,768,32]{2,3,1,0:T(8,128)}, f32[2,2,3072,32]{2,3,1,0:T(8,128)}) async-done(((f32[2,4,768,32]{2,3,1,0:T(8,128)}, f32[2,2,3072,32]{2,3,1,0:T(8,128)}), (f32[2,4,768,32]{2,3,1,0:T(8,128)}, f32[2,2,3072,32]{2,3,1,0:T(8,128)})) %all-reduce.11.cloned.1.call-update) | async-done | bytes 2359312 | tf_op jit(solution)/shard_map/psum | solution.py:37
  765.0 1.3 broadcast_multiply_fusion.1
  766.3 0.1 constant_dynamic-slice_fusion.1
  766.4 0.7 copy.113
  767.2 0.7 copy_subtract_fusion.1
  767.9 0.9 copy.116
  768.8 0.9 copy.115
  769.7 0.9 copy.110
  770.6 0.1 broadcast_multiply_fusion
  770.7 0.9 copy-done.7
  771.7 0.2 copy-done.8
  771.8 1.5 copy_subtract_fusion
  773.4 1.3 copy.118
  774.6 1.3 copy.117
  775.9 1.3 copy.111
  777.2 0.7 constant_dynamic-slice_fusion
  (19 shorter events, 0.0 us)
Async XLA Ops:
  7.2 98.0 %all-gather.2.cloned.1.call-start = ((), (), s32[]{:S(2)}) async-start(), calls=%async_computation | async-start | bytes 6389760 | tf_op jit(solution)/shard_map/all_gather | solution.py:75
  8.8 218.2 %all-reduce.17.cloned.1.call-start = ((), (), s32[]{:S(2)}) async-start(), calls=%async_computation.4 | async-start | bytes 4718592 | tf_op jit(solution)/shard_map/psum | solution.py:37
  9.7 59.7 %copy-start.2 = (f32[1,2,4,12,768]{4,2,3,1,0:T(4,128)S(1)}, f32[1,2,4,12,768]{4,2,3,1,0:T(4,128)}, u32[]{:S(2)}) copy-start(f32[1,2,4,12,768]{4,2,3,1,0:T(4,128)} %param.16) | copy-start | bytes 884740
  9.7 59.7 %copy-start.3 = (bf16[1,2,4,12,768]{4,2,3,1,0:T(4,128)(2,1)S(1)}, bf16[1,2,4,12,768]{4,2,3,1,0:T(4,128)(2,1)}, u32[]{:S(2)}) copy-start(bf16[1,2,4,12,768]{4,2,3,1,0:T(4,128)(2,1)} %param.15) | copy-start | bytes 442372
  69.4 35.8 %copy-start = (f32[1,2,2,12,3072]{4,2,3,1,0:T(2,128)S(1)}, f32[1,2,2,12,3072]{4,2,3,1,0:T(2,128)}, u32[]{:S(2)}) copy-start(f32[1,2,2,12,3072]{4,2,3,1,0:T(2,128)} %param.22) | copy-start | bytes 1769476
  69.4 35.8 %copy-start.1 = (bf16[1,2,2,12,3072]{4,2,3,1,0:T(2,128)(2,1)S(1)}, bf16[1,2,2,12,3072]{4,2,3,1,0:T(2,128)(2,1)}, u32[]{:S(2)}) copy-start(bf16[1,2,2,12,3072]{4,2,3,1,0:T(2,128)(2,1)} %param.21) | copy-start | bytes 884740
  71.5 63.5 %copy-start.11 = (f32[2,4,3,32,32]{4,3,2,1,0:T(8,128)S(1)}, f32[2,4,3,32,32]{4,3,2,1,0:T(8,128)}, u32[]{:S(2)}) copy-start(f32[2,4,3,32,32]{4,3,2,1,0:T(8,128)} %param.18) | copy-start | bytes 294916
  111.3 25.7 %copy-start.12 = (f32[2,2,3,32,32]{4,3,2,1,0:T(8,128)S(1)}, f32[2,2,3,32,32]{4,3,2,1,0:T(8,128)}, u32[]{:S(2)}) copy-start(f32[2,2,3,32,32]{4,3,2,1,0:T(8,128)} %param.24) | copy-start | bytes 147460
  140.0 87.2 %copy-start.15 = (bf16[1,2,156]{2,1,0:T(2,128)(2,1)S(1)}, bf16[1,2,156]{2,1,0:T(2,128)(2,1)}, u32[]{:S(2)}) copy-start(bf16[1,2,156]{2,1,0:T(2,128)(2,1)} %param.27) | copy-start | bytes 1876
  140.0 293.3 %all-reduce.13.cloned.1.call-start = ((), (), s32[]{:S(2)}) async-start(), calls=%async_computation.2 | async-start | bytes 4718592 | tf_op jit(solution)/shard_map/psum | solution.py:37
  227.0 331.9 %all-reduce.15.cloned.1.call-start = ((), (), s32[]{:S(2)}) async-start(), calls=%async_computation.3 | async-start | bytes 4718592 | tf_op jit(solution)/shard_map/psum | solution.py:37
  433.3 2.9 copy-start.6
  468.8 91.5 %copy-start.13 = (f32[2,156]{1,0:T(2,128)S(1)}, f32[2,156]{1,0:T(2,128)}, u32[]{:S(2)}) copy-start(f32[2,156]{1,0:T(2,128)} %param.29) | copy-start | bytes 3748
  468.8 91.5 %copy-start.14 = (f32[2,156]{1,0:T(2,128)S(1)}, f32[2,156]{1,0:T(2,128)}, u32[]{:S(2)}) copy-start(f32[2,156]{1,0:T(2,128)} %param.28) | copy-start | bytes 3748
  468.8 296.2 %all-reduce.11.cloned.1.call-start = ((), (), s32[]{:S(2)}) async-start(), calls=%async_computation.1 | async-start | bytes 4718592 | tf_op jit(solution)/shard_map/psum | solution.py:37
  559.0 208.2 %copy-start.9 = (f32[2,4,12,768]{3,1,2,0:T(4,128)S(1)}, f32[2,4,12,768]{3,1,2,0:T(4,128)}, u32[]{:S(2)}) copy-start(f32[2,4,12,768]{3,1,2,0:T(4,128)} %param.20) | copy-start | bytes 884740
  559.0 208.2 %copy-start.10 = (f32[2,4,12,768]{3,1,2,0:T(4,128)S(1)}, f32[2,4,12,768]{3,1,2,0:T(4,128)}, u32[]{:S(2)}) copy-start(f32[2,4,12,768]{3,1,2,0:T(4,128)} %param.19) | copy-start | bytes 884740
  765.0 2.1 copy-start.5
  767.9 2.7 copy-start.4
  770.6 1.1 copy-start.7
  770.6 1.2 copy-start.8
Sparse Core Ops, SparseCore 0:
  11.9 93.1 all-gather.1
  140.1 86.7 all-reduce.16
  230.6 202.6 all-reduce.12
  468.9 89.9 all-reduce.14
  562.4 202.6 all-reduce.10
